TPU v7x, 32 devices: a whole 2x2x4 slice. The times are simulated.
32 devices in a mesh: plane: 4 (over y, core), frame: 8 (over z, x).
Axes of the slice: x: 2, y: 2, z: 4, core: 2. Of those that a mesh axis runs over, the one named last changes fastest.
Arguments:
- image: float32 [8, 8, 2, 128, 128], P('plane', 'frame'), may hold values from -6 to 6
- sens: bfloat16 [4, 8, 2, 128, 128], P(None, 'plane'), may hold values from -3 to 3
- kspace: bfloat16 [4, 8, 8, 2, 128, 128], P(None, 'plane', 'frame'), may hold values from -6 to 6
- offsets: int32 [8, 128], P('frame'), may hold values from 0 to 3
- shifts: int32 [2], replicated, may hold values from 0 to 7
- step_size: float32 [1], replicated, may hold values from 0.5 to 1.5
- threshold: float32 [1], replicated, may hold values from 100 to 1000
Outputs:
- new_image: float32 [8, 8, 2, 128, 128], P('plane', 'frame')
All inputs are finite; a program needn't handle non-finite values.
Results may differ from a plain program's by a relative error of at most 0.0003.
Values sent between devices are 32-bit elements; how exact they have to be, the bound alone decides.
A program may use at most 64 MiB of HBM per device.

v0:
```python
import math
import jax
import jax.numpy as jnp
from jax import lax
from jax.sharding import PartitionSpec as P

PATCH_Y = 8
PATCH_Z = 8
ACCEL = 4
CENTER = 8


def from_partner(block, axis, distance):
    count = lax.axis_size(axis)
    route = []
    for low in range(count):
        high = low | 1 << distance
        if high != low and high < count:
            route += [(low, high), (high, low)]
    return lax.ppermute(block, axis, route)


def dft_tables(length):
    indices = jnp.arange(length, dtype=jnp.int32)
    phases = indices[:, None] * indices[None, :] % length
    angles = phases.astype(jnp.float32) * (2.0 * math.pi / length)
    norm_scale = 1.0 / math.sqrt(length)
    return (jnp.cos(angles) * norm_scale, jnp.sin(angles) * norm_scale)


def along_z(stacked, right_table, sign, width_z):
    product = jnp.einsum(
        "...z,zw->...w",
        stacked,
        right_table,
        precision=lax.Precision.HIGHEST,
        preferred_element_type=jnp.float32,
    )
    cos_part = product[..., :width_z]
    sin_part = product[..., width_z:]
    real_part = cos_part[..., 0, :, :] + sign * sin_part[..., 1, :, :]
    imag_part = cos_part[..., 1, :, :] - sign * sin_part[..., 0, :, :]
    return jnp.stack([real_part, imag_part], axis=-3)


def along_y(stacked, left_table):
    shape_in = stacked.shape
    merged = stacked.reshape(shape_in[:-3] + (2 * shape_in[-2], shape_in[-1]))
    result = jnp.einsum(
        "ur,...rz->...uz",
        left_table,
        merged,
        precision=lax.Precision.HIGHEST,
        preferred_element_type=jnp.float32,
    )
    return result.reshape(shape_in)


def rotate(casorati):
    frames2, voxels = (casorati.shape[-2], casorati.shape[-1])
    split_parts = casorati.reshape(casorati.shape[:-2] + (frames2 // 2, 2, voxels))
    turned = jnp.stack([-split_parts[..., 1, :], split_parts[..., 0, :]], axis=-2)
    return turned.reshape(casorati.shape)


def gram_of(casorati):
    twin = rotate(casorati)
    first = jnp.einsum(
        "kav,kbv->kab",
        casorati,
        casorati,
        precision=lax.Precision.HIGHEST,
        preferred_element_type=jnp.float32,
    )
    second = jnp.einsum(
        "kav,kbv->kab",
        twin,
        twin,
        precision=lax.Precision.HIGHEST,
        preferred_element_type=jnp.float32,
    )
    return first + second


def shrink(casorati, gram, level):
    order = gram.shape[-1]
    system = gram + level * jnp.eye(order, dtype=jnp.float32)
    factor = jnp.linalg.cholesky(system)
    forward_part = jax.scipy.linalg.solve_triangular(factor, casorati, lower=True)
    solved = jax.scipy.linalg.solve_triangular(factor, forward_part, lower=True, trans=1)
    return casorati - level * solved


def local(image, sens, kspace, offsets, shifts, step_size, threshold):
    planes, frames_dev, _, width_y, width_z = image.shape
    frames = frames_dev * lax.axis_size("frame")
    cos_y, sin_y = dft_tables(width_y)
    cos_z, sin_z = dft_tables(width_z)
    right_table = jnp.concatenate([cos_z, sin_z], axis=1)
    left_forward = jnp.concatenate(
        [jnp.concatenate([cos_y, sin_y], axis=1), jnp.concatenate([-sin_y, cos_y], axis=1)], axis=0
    )
    left_inverse = jnp.concatenate(
        [jnp.concatenate([cos_y, -sin_y], axis=1), jnp.concatenate([sin_y, cos_y], axis=1)], axis=0
    )
    rows_y = jnp.arange(width_y, dtype=jnp.int32)
    rows_z = jnp.arange(width_z, dtype=jnp.int32)
    low_y = (rows_y < CENTER) | (rows_y >= width_y - CENTER)
    low_z = (rows_z < CENTER) | (rows_z >= width_z - CENTER)
    regular = (rows_z[None, None, :] + offsets[:, :, None]) % ACCEL == 0
    sampled = (regular | low_y[None, :, None] & low_z[None, None, :]).astype(jnp.float32)
    image_re = image[:, :, 0]
    image_im = image[:, :, 1]
    maps = sens.astype(jnp.float32)
    sens_re = maps[:, :, 0][:, :, None]
    sens_im = maps[:, :, 1][:, :, None]
    coil_re = sens_re * image_re[None] - sens_im * image_im[None]
    coil_im = sens_re * image_im[None] + sens_im * image_re[None]
    stacked = jnp.stack([coil_re, coil_im], axis=3)
    spectra = along_y(along_z(stacked, right_table, 1.0, width_z), left_forward)
    resid = sampled[None, None, :, None] * (spectra - kspace.astype(jnp.float32))
    returned = along_z(along_y(resid, left_inverse), right_table, -1.0, width_z)
    back_re = returned[:, :, :, 0]
    back_im = returned[:, :, :, 1]
    grad_re = jnp.sum(sens_re * back_re + sens_im * back_im, axis=0)
    grad_im = jnp.sum(sens_re * back_im - sens_im * back_re, axis=0)
    moved = image - step_size[0] * jnp.stack([grad_re, grad_im], axis=2)
    rolled = jnp.roll(moved, (shifts[0], shifts[1]), axis=(3, 4))
    nyb = width_y // PATCH_Y
    nzb = width_z // PATCH_Z
    voxels = planes * PATCH_Y * PATCH_Z
    blocks = rolled.reshape(planes, frames_dev, 2, nyb, PATCH_Y, nzb, PATCH_Z)
    blocks = blocks.transpose(3, 5, 1, 2, 0, 4, 6).reshape(nyb * nzb, frames_dev, 2, voxels)
    regrouped = lax.all_to_all(blocks, "frame", split_axis=0, concat_axis=1, tiled=True)
    count = regrouped.shape[0]
    casorati = regrouped.reshape(count, 2 * frames, voxels)
    level = threshold[0]
    parity = lax.axis_index("plane") % 2
    halfway = count // 2
    first_part = casorati[:halfway]
    second_part = casorati[halfway:]
    kept_part = jnp.where(parity == 0, first_part, second_part)
    outgoing = jnp.where(parity == 0, second_part, first_part)
    incoming = from_partner(outgoing, "plane", 0)
    complete = jnp.concatenate([kept_part, incoming], axis=2)
    finished = shrink(complete, gram_of(complete), level)
    own_part = finished[:, :, :voxels]
    returned_part = from_partner(finished[:, :, voxels:], "plane", 0)
    shrunk = jnp.where(
        parity == 0,
        jnp.concatenate([own_part, returned_part], axis=0),
        jnp.concatenate([returned_part, own_part], axis=0),
    )
    restored = lax.all_to_all(
        shrunk.reshape(count, frames, 2, voxels), "frame", split_axis=1, concat_axis=0, tiled=True
    )
    placed = restored.reshape(nyb, nzb, frames_dev, 2, planes, PATCH_Y, PATCH_Z)
    placed = placed.transpose(4, 2, 3, 0, 5, 1, 6).reshape(planes, frames_dev, 2, width_y, width_z)
    return jnp.roll(placed, (-shifts[0], -shifts[1]), axis=(3, 4))


def solution(mesh):
    in_specs = (
        P("plane", "frame", None, None, None),
        P(None, "plane", None, None, None),
        P(None, "plane", "frame", None, None, None),
        P("frame", None),
        P(),
        P(),
        P(),
    )
    out_specs = P("plane", "frame", None, None, None)
    return jax.shard_map(local, mesh=mesh, in_specs=in_specs, out_specs=out_specs, check_vma=False)
```

profile of v0, /device:TPU:0, one launch (start us, length us, event | category | flops | bytes accessed | tf_op | source)
XLA Modules:
  0.0 114.0 jit_solution(13654522863200061980)
XLA Ops:
  0.0 1.3 %fusion.51 = (s32[1]{0:T(128)}, s32[1]{0:T(128)}) fusion(s32[2]{0:T(128)} %param.13), kind=kLoop, calls=%fused_computation.107 | loop fusion | bytes 16 | tf_op jit(solution)/shard_map/jit(_roll_dynamic)/unstack | solution.py:128
  3.2 0.3 sine_multiply_fusion
  3.5 0.3 fusion.44
  5.6 1.1 copy_convert_fusion
  6.8 1.0 slice_bitcast_fusion.1
  7.8 0.1 subtract_bitcast_fusion
  7.9 1.8 %convolution_bitcast_fusion.1 = f32[4,2,1,2,128,256]{5,4,3,1,0,2:T(8,128)S(1)} fusion(f32[4,2,1,1,128,128]{5,4,3,1,0,2:T(8,128)S(1)} %get-tuple-element.11, f32[4,2,1,1,128,128]{5,4,3,1,0,2:T(8,128)S(1)} %get-tuple-element.10, f32[128,128]{1,0:T(8,128)S(1)} %get-tuple-element.24, f32[128,128]{1,0:T(8,128)S(1)} %get-tuple-element.25), kind=kOutput, calls=%fused_computation.1 | convolution fusion | flops 805601280 | bytes 3276800 | tf_op jit(solution)/shard_map/...z,zw->...w/dot_general | solution.py:32
  9.7 0.1 slice_add_fusion
  9.8 0.1 pad_maximum_fusion
  9.9 0.0 copy-start.1
  9.9 1.8 %convolution_bitcast_fusion.3 = f32[4,2,1,256,128]{3,4,1,0,2:T(8,128)S(1)} fusion(f32[4,2,256,128]{3,2,1,0:T(8,128)S(1)} %bitcast.121, f32[128,128]{1,0:T(8,128)S(1)} %get-tuple-element.25, f32[128,128]{1,0:T(8,128)S(1)} %fusion.44, f32[128,128]{1,0:T(8,128)S(1)} %get-tuple-element.24), kind=kOutput, calls=%fused_computation.3 | convolution fusion | flops 805502976 | bytes 2293760 | tf_op jit(solution)/shard_map/ur,...rz->...uz/dot_general | solution.py:49
  11.7 0.3 copy.101
  12.1 0.0 copy-done.1
  12.1 0.1 fusion.43
  12.2 1.2 %subtract_multiply_fusion = f32[4,2,1,2,128,128]{5,4,3,2,1,0:T(8,128)S(1)} fusion(f32[4,2,1,2,128,128]{5,4,3,2,1,0:T(8,128)S(1)} %bitcast.122, bf16[4,2,1,2,128,128]{5,4,3,2,1,0:T(8,128)(2,1)} %param.11, f32[128,128]{1,0:T(8,128)S(1)} %fusion.43), kind=kLoop, calls=%fused_computation.12 | loop fusion | flops 786432 | bytes 2686976 | tf_op jit(solution)/shard_map/mul | solution.py:121
  13.4 1.8 %convolution_bitcast_fusion.2 = f32[4,2,1,256,128]{3,4,1,0,2:T(8,128)S(1)} fusion(f32[4,2,256,128]{3,2,1,0:T(8,128)S(1)} %bitcast.123, f32[128,128]{1,0:T(8,128)S(1)} %get-tuple-element.25, f32[128,128]{1,0:T(8,128)S(1)} %get-tuple-element.24, f32[128,128]{1,0:T(8,128)S(1)} %fusion.44), kind=kOutput, calls=%fused_computation.2 | convolution fusion | flops 805502976 | bytes 2293760 | tf_op jit(solution)/shard_map/ur,...rz->...uz/dot_general | solution.py:49
  15.2 0.3 copy.102
  15.5 1.8 %convolution_bitcast_fusion = f32[4,2,1,2,128,256]{5,4,1,0,3,2:T(8,128)S(1)} fusion(f32[4,2,2,128,128]{4,3,2,1,0:T(8,128)S(1)} %bitcast.120, f32[128,128]{1,0:T(8,128)S(1)} %get-tuple-element.24, f32[128,128]{1,0:T(8,128)S(1)} %get-tuple-element.25), kind=kOutput, calls=%fused_computation | convolution fusion | flops 805339136 | bytes 3276800 | tf_op jit(solution)/shard_map/...z,zw->...w/dot_general | solution.py:32
  17.4 0.0 copy-start
  17.4 0.3 add_reduce_fusion
  18.3 0.0 copy-done
  18.3 0.1 fusion.18
  18.4 0.2 fusion.17
  18.7 3.6 %reshape.304 = f32[2,1,2,16,8,16,8]{6,5,4,3,2,0,1:T(8,128)} reshape(f32[2,1,2,128,128]{4,3,2,1,0:T(8,128)S(1)} %fusion.17) | data formatting | bytes 524288 | tf_op jit(solution)/shard_map/reshape | solution.py:132
  22.3 2.9 %copy.73 = f32[16,16,1,2,2,8,8]{1,0,6,5,4,3,2:T(8,128)S(1)} copy(f32[16,16,1,2,2,8,8]{6,1,5,0,3,4,2:T(8,128)} %bitcast.118) | data formatting | bytes 524288 | tf_op jit(solution)/shard_map/transpose | solution.py:133
  25.2 0.9 reshape.305
  26.1 0.8 copy.74
  27.0 7.3 %all-to-all-start = ((f32[256,1,2,128]{3,2,1,0:T(2,128)}), f32[256,1,2,128]{3,2,1,0:T(2,128)S(1)}, u32[]{:S(2)}, u32[]{:S(2)}) async-start(f32[256,1,2,128]{3,2,1,0:T(2,128)} %copy.74), calls=%async_computation | async-start | bytes 524288 | tf_op jit(solution)/shard_map/all_to_all | solution.py:134
  34.9 8.2 %all-to-all-done = f32[256,1,2,128]{3,2,1,0:T(2,128)S(1)} async-done(((f32[256,1,2,128]{3,2,1,0:T(2,128)}), f32[256,1,2,128]{3,2,1,0:T(2,128)S(1)}, u32[]{:S(2)}, u32[]{:S(2)}) %all-to-all-start) | async-done | bytes 262176 | tf_op jit(solution)/shard_map/all_to_all | solution.py:134
  43.2 0.1 copy.77
  43.3 0.1 collective-permute-start
  43.4 0.1 copy.80
  43.5 0.1 copy.76
  43.6 1.1 collective-permute-done
  44.8 0.1 reshape.306
  44.9 0.2 slice_negate_fusion
  45.1 0.2 pad_maximum_fusion.8
  45.4 0.2 reshape.307
  45.6 0.4 fusion.52
  45.9 0.4 broadcast_add_fusion
  46.3 0.1 copy.81
  46.4 23.5 %custom-call.11 = f32[16,16,16]{2,1,0:T(8,128)S(1)} custom-call(f32[16,16,16]{2,1,0:T(8,128)S(1)} %fusion.30), custom_call_target="Cholesky" | custom-call | tf_op jit(solution)/shard_map/jit(cholesky)/cholesky | solution.py:88
  69.9 0.1 compare_reduce_fusion
  70.1 0.1 select_bitcast_fusion
  70.2 19.8 %custom-call.12 = f32[16,1,16,16]{2,3,1,0:T(8,128)S(1)} custom-call(f32[16,1,16,16]{3,2,1,0:T(8,128)S(1)} %select_bitcast_fusion), custom_call_target="InvertDiagBlocksLowerTriangular" | custom-call | tf_op jit(solution)/shard_map/jit(_solve_triangular)/vmap()/triangular_solve | solution.py:90
  89.9 0.5 fusion.27
  90.4 0.4 fusion
  90.8 0.2 collective-permute-start.1
  91.1 1.2 %collective-permute-done.1 = f32[16,16,128]{2,1,0:T(8,128)S(1)} collective-permute-done((f32[16,16,128]{2,1,0:T(8,128)S(1)}, f32[16,16,128]{2,1,0:T(8,128)S(1)}, u32[]{:S(2)}, u32[]{:S(2)}) %collective-permute-start.1) | collective-permute-done | bytes 131104 | tf_op jit(solution)/shard_map/ppermute | solution.py:20
  92.3 0.7 maximum_select_fusion
  93.0 3.6 %all-to-all-start.1 = ((f32[32,8,2,128]{3,0,2,1:T(8,128)}), f32[32,8,2,128]{3,0,2,1:T(8,128)S(1)}, u32[]{:S(2)}, u32[]{:S(2)}) async-start(f32[32,8,2,128]{3,0,2,1:T(8,128)} %maximum_select_fusion), calls=%async_computation.1 | async-start | bytes 524288 | tf_op jit(solution)/shard_map/all_to_all | solution.py:154
  97.9 8.0 %all-to-all-done.1 = f32[32,8,2,128]{3,0,2,1:T(8,128)S(1)} async-done(((f32[32,8,2,128]{3,0,2,1:T(8,128)}), f32[32,8,2,128]{3,0,2,1:T(8,128)S(1)}, u32[]{:S(2)}, u32[]{:S(2)}) %all-to-all-start.1) | async-done | bytes 262176 | tf_op jit(solution)/shard_map/all_to_all | solution.py:154
  105.9 0.4 copy.87
  106.3 0.3 reshape.308
  106.6 2.8 %copy.88 = f32[2,1,2,16,8,16,8]{6,5,4,3,2,0,1:T(8,128)} copy(f32[2,1,2,16,8,16,8]{5,3,6,4,0,2,1:T(8,128)S(1)} %bitcast.119) | data formatting | bytes 524288 | tf_op jit(solution)/shard_map/transpose | solution.py:158
  109.4 3.6 %reshape.309 = f32[2,1,2,128,128]{4,3,2,0,1:T(8,128)S(1)} reshape(f32[2,1,2,16,8,16,8]{6,5,4,3,2,0,1:T(8,128)} %copy.88) | data formatting | bytes 524288 | tf_op jit(solution)/shard_map/reshape | solution.py:158
  113.0 0.1 fusion.16
  113.1 0.9 fusion.15
  (13 shorter events, 0.3 us)
Async XLA Ops:
  9.9 2.2 %copy-start.1 = (s32[1,128]{1,0:T(1,128)S(1)}, s32[1,128]{1,0:T(1,128)}, u32[]{:S(2)}) copy-start(s32[1,128]{1,0:T(1,128)} %param.12) | copy-start | bytes 1540
  17.4 1.0 copy-start
  27.0 16.2 %all-to-all-start = ((f32[256,1,2,128]{3,2,1,0:T(2,128)}), f32[256,1,2,128]{3,2,1,0:T(2,128)S(1)}, u32[]{:S(2)}, u32[]{:S(2)}) async-start(f32[256,1,2,128]{3,2,1,0:T(2,128)} %copy.74), calls=%async_computation | async-start | bytes 524288 | tf_op jit(solution)/shard_map/all_to_all | solution.py:134
  43.3 1.4 %collective-permute-start = (f32[16,16,128]{2,1,0:T(8,128)S(1)}, f32[16,16,128]{2,1,0:T(8,128)S(1)}, u32[]{:S(2)}, u32[]{:S(2)}) collective-permute-start(f32[16,16,128]{2,1,0:T(8,128)S(1)} %bitcast.133), channel_id=1, source_target_pairs={{0,8},{8,0},{16,24},{24,16},{1,9},{9,1},{17,25},{25,17},{2,10},{10... | collective-permute-start | bytes 393224 | tf_op jit(solution)/shard_map/ppermute | solution.py:20
  90.8 1.4 %collective-permute-start.1 = (f32[16,16,128]{2,1,0:T(8,128)S(1)}, f32[16,16,128]{2,1,0:T(8,128)S(1)}, u32[]{:S(2)}, u32[]{:S(2)}) collective-permute-start(f32[16,16,128]{2,1,0:T(8,128)S(1)} %get-tuple-element.13), channel_id=1, source_target_pairs={{0,8},{8,0},{16,24},{24,16},{1,9},{9,1},{17,25},{25,17},{2,10},{10... | collective-permute-start | bytes 393224 | tf_op jit(solution)/shard_map/ppermute | solution.py:20
  93.0 12.9 %all-to-all-start.1 = ((f32[32,8,2,128]{3,0,2,1:T(8,128)}), f32[32,8,2,128]{3,0,2,1:T(8,128)S(1)}, u32[]{:S(2)}, u32[]{:S(2)}) async-start(f32[32,8,2,128]{3,0,2,1:T(8,128)} %maximum_select_fusion), calls=%async_computation.1 | async-start | bytes 524288 | tf_op jit(solution)/shard_map/all_to_all | solution.py:154
where the time goes:
time: 115 us; the launch traced here: 114 us
  other arithmetic  49.6 us (43%)
  local copies, waits for them, and re-layouts  19.3 us (17%)
  waiting for transfers between devices  18.5 us (16%)
  starting transfers between devices  11.2 us (10%)
  matrix products  8.81 us (8%)
  between operations  6.67 us (6%)
    another operation x4, other arithmetic, shrink(): factor = jnp.linalg.cholesky(system)  23.6 us
    another operation x3, other arithmetic, shrink(): jax.scipy.linalg.solve_triangular(factor, forward_part, lower=True, trans=1)  19.9 us
    all_to_all x1, waiting for transfers between devices, local(): lax.all_to_all(blocks, 'frame', split_axis=0, concat_axis=1, tiled=True)  8.25 us
    all_to_all x1, waiting for transfers between devices, local(): lax.all_to_all(shrunk.reshape(count, frames, 2, voxels), 'frame', split_a...  8.01 us
    all_to_all x1, starting transfers between devices, local(): lax.all_to_all(blocks, 'frame', split_axis=0, concat_axis=1, tiled=True)  7.29 us
    reshape x1, local copies, waits for them, and re-layouts, local(): placed.transpose(4, 2, 3, 0, 5, 1, 6)  3.64 us
    dot_general x2, matrix products, along_y(): jnp.einsum('ur,...rz->...uz', left_table, merged, precision=lax.Precision...  3.62 us
    reshape x1, local copies, waits for them, and re-layouts, local(): blocks = rolled.reshape(planes, frames_dev, 2, nyb, PATCH_Y, nzb, PATCH_Z)  3.62 us
  transfers between devices with their start and end apart: 4, of which 4 were waited for; matrix products, arithmetic and copies ran while one was open for 0% of the time, Pallas kernels for 0%

commit v1 on v0

--- a/solution.py
+++ b/solution.py
@@ -151,8 +151,16 @@
         jnp.concatenate([own_part, returned_part], axis=0),
         jnp.concatenate([returned_part, own_part], axis=0),
     )
-    restored = lax.all_to_all(
-        shrunk.reshape(count, frames, 2, voxels), "frame", split_axis=1, concat_axis=0, tiled=True
+    restored = jnp.concatenate(
+        lax.all_to_all(
+            jnp.stack(
+                jnp.split(shrunk.reshape(count, frames, 2, voxels), lax.axis_size("frame"), axis=1)
+            ),
+            "frame",
+            0,
+            0,
+        ),
+        axis=0,
     )
     placed = restored.reshape(nyb, nzb, frames_dev, 2, planes, PATCH_Y, PATCH_Z)
     placed = placed.transpose(4, 2, 3, 0, 5, 1, 6).reshape(planes, frames_dev, 2, width_y, width_z)

time: 115 us -> 119 us (1.035)
  local copies, waits for them, and re-layouts: 19.3 us -> 24.3 us
    unnamed x4 -> x11, local copies, waits for them, and re-layouts: 0.02 us -> 4.34 us
where the time goes in v1:
time: 119 us; the launch traced here: 118 us
  other arithmetic  48.9 us (41%)
  local copies, waits for them, and re-layouts  24.3 us (20%)
  waiting for transfers between devices  18.6 us (16%)
  starting transfers between devices  11.2 us (9%)
  matrix products  8.81 us (7%)
  between operations  6.5 us (5%)
    another operation x4, other arithmetic, shrink(): factor = jnp.linalg.cholesky(system)  23.6 us
    another operation x3, other arithmetic, shrink(): jax.scipy.linalg.solve_triangular(factor, forward_part, lower=True, trans=1)  19.9 us
    all_to_all x1, waiting for transfers between devices, local(): lax.all_to_all(blocks, 'frame', split_axis=0, concat_axis=1, tiled=True)  8.25 us
    all_to_all x1, waiting for transfers between devices, local(): lax.all_to_all(jnp.stack(jnp.split(shrunk.reshape(count, frames, 2, voxel...  8.05 us
    all_to_all x1, starting transfers between devices, local(): lax.all_to_all(blocks, 'frame', split_axis=0, concat_axis=1, tiled=True)  7.28 us
    unnamed x11, local copies, waits for them, and re-layouts  4.34 us
    reshape x1, local copies, waits for them, and re-layouts, local(): placed.transpose(4, 2, 3, 0, 5, 1, 6)  3.64 us
    dot_general x2, matrix products, along_y(): jnp.einsum('ur,...rz->...uz', left_table, merged, precision=lax.Precision...  3.62 us
  transfers between devices with their start and end apart: 4, of which 4 were waited for; matrix products, arithmetic and copies ran while one was open for 0% of the time, Pallas kernels for 0%

profile of v1, /device:TPU:0, one launch (start us, length us, event | category | flops | bytes accessed | tf_op | source)
XLA Modules:
  0.0 118.3 jit_solution(6855452954320251593)
XLA Ops:
  0.0 1.3 %fusion.52 = (s32[1]{0:T(128)}, s32[1]{0:T(128)}) fusion(s32[2]{0:T(128)} %param.13), kind=kLoop, calls=%fused_computation.116 | loop fusion | bytes 16 | tf_op jit(solution)/shard_map/jit(_roll_dynamic)/unstack | solution.py:128
  3.0 0.3 sine_multiply_fusion
  3.3 0.3 fusion.44
  5.5 1.1 copy_convert_fusion
  6.6 1.0 slice_bitcast_fusion.1
  7.6 0.1 subtract_bitcast_fusion
  7.7 1.8 %convolution_bitcast_fusion.1 = f32[4,2,1,2,128,256]{5,4,3,1,0,2:T(8,128)S(1)} fusion(f32[4,2,1,1,128,128]{5,4,3,1,0,2:T(8,128)S(1)} %get-tuple-element.11, f32[4,2,1,1,128,128]{5,4,3,1,0,2:T(8,128)S(1)} %get-tuple-element.10, f32[128,128]{1,0:T(8,128)S(1)} %get-tuple-element.32, f32[128,128]{1,0:T(8,128)S(1)} %get-tuple-element.33), kind=kOutput, calls=%fused_computation.1 | convolution fusion | flops 805601280 | bytes 3276800 | tf_op jit(solution)/shard_map/...z,zw->...w/dot_general | solution.py:32
  9.5 0.1 slice_add_fusion
  9.7 0.1 pad_maximum_fusion
  9.7 0.0 copy-start.1
  9.7 1.8 %convolution_bitcast_fusion.3 = f32[4,2,1,256,128]{3,4,1,0,2:T(8,128)S(1)} fusion(f32[4,2,256,128]{3,2,1,0:T(8,128)S(1)} %bitcast.126, f32[128,128]{1,0:T(8,128)S(1)} %get-tuple-element.33, f32[128,128]{1,0:T(8,128)S(1)} %fusion.44, f32[128,128]{1,0:T(8,128)S(1)} %get-tuple-element.32), kind=kOutput, calls=%fused_computation.3 | convolution fusion | flops 805502976 | bytes 2293760 | tf_op jit(solution)/shard_map/ur,...rz->...uz/dot_general | solution.py:49
  11.6 0.3 copy.130
  11.9 0.1 fusion.43
  12.0 1.2 subtract_multiply_fusion
  13.2 1.8 %convolution_bitcast_fusion.2 = f32[4,2,1,256,128]{3,4,1,0,2:T(8,128)S(1)} fusion(f32[4,2,256,128]{3,2,1,0:T(8,128)S(1)} %bitcast.128, f32[128,128]{1,0:T(8,128)S(1)} %get-tuple-element.33, f32[128,128]{1,0:T(8,128)S(1)} %get-tuple-element.32, f32[128,128]{1,0:T(8,128)S(1)} %fusion.44), kind=kOutput, calls=%fused_computation.2 | convolution fusion | flops 805502976 | bytes 2293760 | tf_op jit(solution)/shard_map/ur,...rz->...uz/dot_general | solution.py:49
  15.0 0.3 copy.131
  15.4 1.8 %convolution_bitcast_fusion = f32[4,2,1,2,128,256]{5,4,1,0,3,2:T(8,128)S(1)} fusion(f32[4,2,2,128,128]{4,3,2,1,0:T(8,128)S(1)} %bitcast.125, f32[128,128]{1,0:T(8,128)S(1)} %get-tuple-element.32, f32[128,128]{1,0:T(8,128)S(1)} %get-tuple-element.33), kind=kOutput, calls=%fused_computation | convolution fusion | flops 805339136 | bytes 3276800 | tf_op jit(solution)/shard_map/...z,zw->...w/dot_general | solution.py:32
  17.2 0.3 add_reduce_fusion
  18.1 0.0 copy-done
  18.2 0.1 fusion.18
  18.3 0.2 fusion.17
  18.5 3.6 %reshape.300 = f32[2,1,2,16,8,16,8]{6,5,4,3,2,0,1:T(8,128)} reshape(f32[2,1,2,128,128]{4,3,2,1,0:T(8,128)S(1)} %fusion.17) | data formatting | bytes 524288 | tf_op jit(solution)/shard_map/reshape | solution.py:132
  22.1 2.9 %copy.94 = f32[16,16,1,2,2,8,8]{1,0,6,5,4,3,2:T(8,128)S(1)} copy(f32[16,16,1,2,2,8,8]{6,1,5,0,3,4,2:T(8,128)} %bitcast.123) | data formatting | bytes 524288 | tf_op jit(solution)/shard_map/transpose | solution.py:133
  25.0 0.9 reshape.301
  26.0 0.8 copy.95
  26.8 7.3 %all-to-all-start = ((f32[256,1,2,128]{3,2,1,0:T(2,128)}), f32[256,1,2,128]{3,2,1,0:T(2,128)S(1)}, u32[]{:S(2)}, u32[]{:S(2)}) async-start(f32[256,1,2,128]{3,2,1,0:T(2,128)} %copy.95), calls=%async_computation | async-start | bytes 524288 | tf_op jit(solution)/shard_map/all_to_all | solution.py:134
  34.7 8.3 %all-to-all-done = f32[256,1,2,128]{3,2,1,0:T(2,128)S(1)} async-done(((f32[256,1,2,128]{3,2,1,0:T(2,128)}), f32[256,1,2,128]{3,2,1,0:T(2,128)S(1)}, u32[]{:S(2)}, u32[]{:S(2)}) %all-to-all-start) | async-done | bytes 262176 | tf_op jit(solution)/shard_map/all_to_all | solution.py:134
  43.1 0.1 copy.98
  43.2 0.1 collective-permute-start
  43.3 0.1 copy.101
  43.3 0.1 copy.97
  43.4 1.1 collective-permute-done
  44.6 0.1 reshape.302
  44.8 0.2 slice_negate_fusion
  45.0 0.2 pad_maximum_fusion.8
  45.2 0.2 reshape.303
  45.4 0.4 fusion.53
  45.8 0.4 broadcast_add_fusion
  46.1 0.1 copy.102
  46.3 23.5 %custom-call.11 = f32[16,16,16]{2,1,0:T(8,128)S(1)} custom-call(f32[16,16,16]{2,1,0:T(8,128)S(1)} %fusion.30), custom_call_target="Cholesky" | custom-call | tf_op jit(solution)/shard_map/jit(cholesky)/cholesky | solution.py:88
  69.8 0.1 compare_reduce_fusion
  69.9 0.1 select_bitcast_fusion
  70.0 19.8 %custom-call.12 = f32[16,1,16,16]{2,3,1,0:T(8,128)S(1)} custom-call(f32[16,1,16,16]{3,2,1,0:T(8,128)S(1)} %select_bitcast_fusion), custom_call_target="InvertDiagBlocksLowerTriangular" | custom-call | tf_op jit(solution)/shard_map/jit(_solve_triangular)/vmap()/triangular_solve | solution.py:90
  89.8 0.5 fusion.27
  90.3 0.4 fusion
  90.7 0.2 collective-permute-start.1
  90.9 1.2 %collective-permute-done.1 = f32[16,16,128]{2,1,0:T(8,128)S(1)} collective-permute-done((f32[16,16,128]{2,1,0:T(8,128)S(1)}, f32[16,16,128]{2,1,0:T(8,128)S(1)}, u32[]{:S(2)}, u32[]{:S(2)}) %collective-permute-start.1) | collective-permute-done | bytes 131104 | tf_op jit(solution)/shard_map/ppermute | solution.py:20
  92.1 0.2 fusion.50
  92.3 0.6 copy_dynamic-update-slice_fusion.7
  92.9 0.6 copy_dynamic-update-slice_fusion.6
  93.5 0.6 copy_dynamic-update-slice_fusion.5
  94.2 0.6 copy_dynamic-update-slice_fusion.4
  94.8 0.6 copy_dynamic-update-slice_fusion.3
  95.4 0.6 copy_dynamic-update-slice_fusion.2
  96.0 0.6 copy_dynamic-update-slice_fusion.1
  96.6 0.6 copy_dynamic-update-slice_fusion
  97.2 3.6 %all-to-all-start.1 = ((f32[8,32,1,2,128]{4,1,3,2,0:T(8,128)}), f32[8,32,1,2,128]{4,1,3,2,0:T(8,128)S(1)}, u32[]{:S(2)}, u32[]{:S(2)}) async-start(f32[8,32,1,2,128]{4,1,3,2,0:T(8,128)} %copy_dynamic-update-slice_fusion), calls=%async_computation.1 | async-start | bytes 524288 | tf_op jit(solution)/shard_map/all_to_all | solution.py:155
  102.1 8.1 %all-to-all-done.1 = f32[8,32,1,2,128]{4,1,3,2,0:T(8,128)S(1)} async-done(((f32[8,32,1,2,128]{4,1,3,2,0:T(8,128)}), f32[8,32,1,2,128]{4,1,3,2,0:T(8,128)S(1)}, u32[]{:S(2)}, u32[]{:S(2)}) %all-to-all-start.1) | async-done | bytes 262176 | tf_op jit(solution)/shard_map/all_to_all | solution.py:155
  110.1 0.4 copy.116
  110.5 0.3 reshape_reshape.3
  110.8 2.8 %copy.117 = f32[2,1,2,16,8,16,8]{6,5,4,3,2,0,1:T(8,128)} copy(f32[2,1,2,16,8,16,8]{5,3,6,4,0,2,1:T(8,128)S(1)} %bitcast.124) | data formatting | bytes 524288 | tf_op jit(solution)/shard_map/transpose | solution.py:166
  113.6 3.6 %reshape.304 = f32[2,1,2,128,128]{4,3,2,0,1:T(8,128)S(1)} reshape(f32[2,1,2,16,8,16,8]{6,5,4,3,2,0,1:T(8,128)} %copy.117) | data formatting | bytes 524288 | tf_op jit(solution)/shard_map/reshape | solution.py:166
  117.3 0.1 fusion.16
  117.3 0.9 fusion.15
  (16 shorter events, 0.2 us)
Async XLA Ops:
  9.7 2.2 %copy-start.1 = (s32[1,128]{1,0:T(1,128)S(1)}, s32[1,128]{1,0:T(1,128)}, u32[]{:S(2)}) copy-start(s32[1,128]{1,0:T(1,128)} %param.12) | copy-start | bytes 1540
  17.2 1.0 copy-start
  26.8 16.2 %all-to-all-start = ((f32[256,1,2,128]{3,2,1,0:T(2,128)}), f32[256,1,2,128]{3,2,1,0:T(2,128)S(1)}, u32[]{:S(2)}, u32[]{:S(2)}) async-start(f32[256,1,2,128]{3,2,1,0:T(2,128)} %copy.95), calls=%async_computation | async-start | bytes 524288 | tf_op jit(solution)/shard_map/all_to_all | solution.py:134
  43.2 1.4 %collective-permute-start = (f32[16,16,128]{2,1,0:T(8,128)S(1)}, f32[16,16,128]{2,1,0:T(8,128)S(1)}, u32[]{:S(2)}, u32[]{:S(2)}) collective-permute-start(f32[16,16,128]{2,1,0:T(8,128)S(1)} %bitcast.145), channel_id=1, source_target_pairs={{0,8},{8,0},{16,24},{24,16},{1,9},{9,1},{17,25},{25,17},{2,10},{10... | collective-permute-start | bytes 393224 | tf_op jit(solution)/shard_map/ppermute | solution.py:20
  90.7 1.4 %collective-permute-start.1 = (f32[16,16,128]{2,1,0:T(8,128)S(1)}, f32[16,16,128]{2,1,0:T(8,128)S(1)}, u32[]{:S(2)}, u32[]{:S(2)}) collective-permute-start(f32[16,16,128]{2,1,0:T(8,128)S(1)} %get-tuple-element.21), channel_id=1, source_target_pairs={{0,8},{8,0},{16,24},{24,16},{1,9},{9,1},{17,25},{25,17},{2,10},{10... | collective-permute-start | bytes 393224 | tf_op jit(solution)/shard_map/ppermute | solution.py:20
  97.2 12.9 %all-to-all-start.1 = ((f32[8,32,1,2,128]{4,1,3,2,0:T(8,128)}), f32[8,32,1,2,128]{4,1,3,2,0:T(8,128)S(1)}, u32[]{:S(2)}, u32[]{:S(2)}) async-start(f32[8,32,1,2,128]{4,1,3,2,0:T(8,128)} %copy_dynamic-update-slice_fusion), calls=%async_computation.1 | async-start | bytes 524288 | tf_op jit(solution)/shard_map/all_to_all | solution.py:155
